TPU v7x, 32 devices: a whole 2x2x4 slice. The times are simulated.
32 devices in a mesh: groups: 2 (over y), row: 4 (over z), col: 4 (over x, core).
Axes of the slice: x: 2, y: 2, z: 4, core: 2. Of those that a mesh axis runs over, the one named last changes fastest.
Arguments:
- green_starting_blocks: float32 [4, 128, 2048], P('groups', None, ('row', 'col')), parts along dimension 0, may hold values from -3 to 3
- fit_vectors: bfloat16 [256, 4096], P('groups'), parts along dimension 0, may hold values from -0.75 to 0.75
- history: bfloat16 [4, 2048, 2048], P('groups', 'row', 'col'), parts along dimension 0, may hold values from -0.125 to 0.125
Outputs:
- green_final: float32 [4, 128, 2048], P('groups', None, ('row', 'col')), parts along dimension 0
There are 2 independent parts, one for each index of `groups`. A program takes and returns all parts, laid end to end along the dimension named above; each array names one. Nothing has to cross between parts.
All inputs are finite; a program needn't handle non-finite values.
Results may differ from a plain program's by a relative error of at most 0.03.
Values may be sent and summed in bfloat16 or wider, within the bound.
A program may use at most 128 MiB of HBM per device.

v0:
```python
import functools

import jax
import jax.numpy as jnp
from jax import lax
from jax.experimental import pallas as pl
from jax.experimental.pallas import tpu as pltpu
from jax.sharding import PartitionSpec as P

NO = 64
NEW = 2
ITERS = 2
PITCH = NO + 8
UL, UR, UB, US, UF = 16, 4, 2, 16, 2
RB, BB, FB = 16, 32, 16
F32 = jnp.float32
BF16 = jnp.bfloat16
MESH = pl.DeviceIdType.MESH
VMEM = pl.BlockSpec(memory_space=pltpu.VMEM)


def mm(a, b):
    return jnp.dot(a, b, preferred_element_type=F32)


def mm_nt(a, b):
    return lax.dot_general(a, b, (((1,), (1,)), ((), ())), preferred_element_type=F32)


def prepare(fit_ref, inner_ref, outer_ref, turned):
    aux = fit_ref.shape[0]
    for pair in range(NO // 2):
        block = fit_ref[:, pair * 2 * NO : (pair + 1) * 2 * NO].astype(F32).T
        for half in range(2):
            i = 2 * pair + half
            piece = block[half * NO : (half + 1) * NO]
            inner_ref[:, i * aux : (i + 1) * aux] = piece.astype(BF16)
            turned[i * PITCH : i * PITCH + NO, :] = piece
    for j in range(NO):
        piece = turned[pl.ds(j, NO, stride=PITCH), :]
        outer_ref[j * aux : (j + 1) * aux, :] = piece.T.astype(BF16)


def products(a, now_ref, inner_ref, outer_ref, g_in, g_out, spread, k_ref):
    aux = inner_ref.shape[1] // NO
    times = now_ref.shape[2] // NO
    rows = times * 2 * NO
    for c in range(2):
        block = now_ref[c, a * NO : (a + 1) * NO, :]
        block_t = block.T
        for n in range(times):
            at = (n * 2 + c) * NO
            g_out[at : at + NO, :] = block[:, n * NO : (n + 1) * NO].astype(BF16)
            g_in[at : at + NO, :] = block_t[n * NO : (n + 1) * NO, :].astype(BF16)

    def left(step, carry):
        lanes = pl.ds(pl.multiple_of(step * 2 * aux, 2 * aux), 2 * aux)
        res = mm(g_in[...], inner_ref[:, lanes])
        spread[pl.ds(2 * step, rows, stride=PITCH), :] = res[:, :aux]
        spread[pl.ds(2 * step + 1, rows, stride=PITCH), :] = res[:, aux:]
        return carry

    lax.fori_loop(0, NO // 2, left, 0, unroll=UL)

    def right(step, carry):
        at = pl.ds(pl.multiple_of(step * RB * aux, aux), RB * aux)
        k_ref[at, :] = mm_nt(outer_ref[at, :], g_out[...]).astype(BF16)
        return carry

    lax.fori_loop(0, NO // RB, right, 0, unroll=UR)


def contract(times, fit_ref, spread, m_ref, k_ref, pi_ref, w_ref):
    aux = fit_ref.shape[0]
    width = 2 * NO
    for n in range(times):

        def bubble(step, acc):
            lhs, rhs = [], []
            for d in range(BB):
                m = BB * step + d
                for c in range(2):
                    at = pl.multiple_of(((n * 2 + c) * NO + m) * PITCH, 8)
                    rhs.append(spread[pl.ds(at, NO), :].astype(BF16))
                m_ref[n * NO + m] = jnp.concatenate(rhs[-2:], axis=0)
                lhs.append(k_ref[pl.ds(pl.multiple_of(m * aux, aux), aux), n * width : (n + 1) * width])
            return acc + mm(jnp.concatenate(lhs, axis=1), jnp.concatenate(rhs, axis=0))

        acc = lax.fori_loop(0, NO // BB, bubble, jnp.zeros((aux, aux), F32), unroll=UB)
        pi_ref[n * aux : (n + 1) * aux, :] = (acc.T * (1.0 / NO)).astype(BF16)

    def screen(step, carry):
        lanes = pl.ds(pl.multiple_of(step * 256, 256), 256)
        w_ref[:, lanes] = mm(pi_ref[...], fit_ref[:, lanes]).astype(BF16)
        return carry

    lax.fori_loop(0, NO * NO // 256, screen, 0, unroll=US)

    scale = (aux * NO) ** (-0.5)
    outs = []
    for n in range(times):

        def final(step, acc):
            at = n * NO + 2 * FB * step
            even = jnp.concatenate([m_ref[at + 2 * d] for d in range(FB)], axis=1)
            odd = jnp.concatenate([m_ref[at + 2 * d + 1] for d in range(FB)], axis=1)
            w = [
                w_ref[n * aux : (n + 1) * aux, pl.ds(pl.multiple_of((FB * step + d) * width, width), width)]
                for d in range(FB)
            ]
            return acc + mm(jnp.concatenate([even, odd], axis=0), jnp.concatenate(w, axis=0))

        acc = lax.fori_loop(0, NO // (2 * FB), final, jnp.zeros((2 * width, width), F32), unroll=UF)
        outs.append((acc[:width, :NO] + acc[width:, NO:]) * scale)
    return jnp.concatenate(outs, axis=1).astype(BF16)


def whole_kernel(
    rows_n, cols_n, green_ref, fit_ref, hist_ref, out_ref,
    inner, outer, turned, g_in, g_out, spread, m_ref, k_ref, pi_ref, w_ref,
    now, energy, seg, part, got, gs_sem, gr_sem, ss_sem, sr_sem,
):
    row, col = lax.axis_index("row"), lax.axis_index("col")
    span = green_ref.shape[2]
    times = span // NO
    source_col = (row * cols_n + col) // rows_n

    def owner(m):
        t = col * rows_n + m
        return t // cols_n, lax.rem(t, cols_n)

    def away(m):
        to_row, to_col = owner(m)
        return jnp.logical_or(to_row != row, to_col != col)

    def foreign(r):
        return jnp.logical_or(row != r, col != source_col)

    def place(r, c):
        return {"row": r, "col": c}

    barrier = pltpu.get_barrier_semaphore()
    for d in range(1, cols_n):
        pl.semaphore_signal(barrier, inc=1, device_id=place(row, lax.rem(col + d, cols_n)), device_id_type=MESH)
    for r in range(rows_n):

        @pl.when(foreign(r))
        def _():
            pl.semaphore_signal(barrier, inc=1, device_id=place(r, source_col), device_id_type=MESH)

    prepare(fit_ref, inner, outer, turned)

    keeps = jnp.where(source_col == col, 1, 0)
    pl.semaphore_wait(barrier, cols_n - 1 + rows_n - keeps)

    def gather(s, d):
        return pltpu.make_async_remote_copy(
            src_ref=energy.at[s],
            dst_ref=seg.at[s, col],
            send_sem=gs_sem.at[s, d],
            recv_sem=gr_sem.at[s, d],
            device_id=place(row, lax.rem(col + d, cols_n)),
            device_id_type=MESH,
        )

    def scatter(s, m):
        return pltpu.make_async_remote_copy(
            src_ref=part.at[s, m],
            dst_ref=got.at[s, row],
            send_sem=ss_sem.at[s, m],
            recv_sem=sr_sem.at[s, row],
            device_id=place(*owner(m)),
            device_id_type=MESH,
        )

    def arriving(s, r):
        return pltpu.make_async_remote_copy(
            src_ref=part.at[s, r],
            dst_ref=got.at[s, r],
            send_sem=ss_sem.at[s, r],
            recv_sem=sr_sem.at[s, r],
            device_id=place(r, source_col),
            device_id_type=MESH,
        )

    def multiply(s):
        for d in range(1, cols_n):
            gather(s, d).wait_recv()
        real = [seg[s, q, :NO, :] for q in range(cols_n)]
        imag = [seg[s, q, NO:, :] for q in range(cols_n)]
        lhs = jnp.concatenate(
            [jnp.concatenate(real + [-x for x in imag], axis=1), jnp.concatenate(imag + real, axis=1)], axis=0
        )
        for m in range(rows_n):
            value = mm(lhs, hist_ref[:, m * span : (m + 1) * span]).astype(BF16)
            part[s, m] = value

            @pl.when(away(m))
            def _():
                scatter(s, m).start()

            @pl.when(jnp.logical_not(away(m)))
            def _():
                got[s, row] = value

    def collect(s, target):
        a = s % NEW
        for r in range(rows_n):

            @pl.when(foreign(r))
            def _():
                arriving(s, r).wait_recv()

        total = got[s, 0].astype(F32)
        for r in range(1, rows_n):
            total = total + got[s, r].astype(F32)
        for c in range(2):
            at = slice(a * NO, (a + 1) * NO)
            target[c, at, :] = green_ref[c, at, :] + total[c * NO : (c + 1) * NO]

    steps = ITERS * NEW
    for s in range(steps):
        a = s % NEW
        if s >= NEW:
            collect(s - NEW, now)
        products(a, green_ref if s < NEW else now, inner, outer, g_in, g_out, spread, k_ref)
        if s >= 1:
            multiply(s - 1)
        value = contract(times, fit_ref, spread, m_ref, k_ref, pi_ref, w_ref)
        energy[s] = value
        for d in range(1, cols_n):
            gather(s, d).start()
        seg[s, col] = value
    multiply(steps - 1)
    for s in range(steps - NEW, steps):
        collect(s, out_ref)
    for s in range(steps):
        for d in range(1, cols_n):
            gather(s, d).wait_send()
        for m in range(rows_n):

            @pl.when(away(m))
            def _():
                scatter(s, m).wait_send()


def local(green, fit, history):
    rows_n, cols_n = lax.axis_size("row"), lax.axis_size("col")
    aux = fit.shape[0]
    span = green.shape[2]
    times = span // NO
    steps = ITERS * NEW
    stacked = history.reshape(2 * history.shape[1], history.shape[2])
    block = (2 * NO, span)
    return pl.pallas_call(
        functools.partial(whole_kernel, rows_n, cols_n),
        out_shape=jax.ShapeDtypeStruct(green.shape, F32),
        in_specs=[VMEM] * 3,
        out_specs=VMEM,
        scratch_shapes=[
            pltpu.VMEM((NO, NO * aux), BF16),
            pltpu.VMEM((NO * aux, NO), BF16),
            pltpu.VMEM((NO * PITCH, aux), F32),
            pltpu.VMEM((times * 2 * NO, NO), BF16),
            pltpu.VMEM((times * 2 * NO, NO), BF16),
            pltpu.VMEM((times * 2 * NO * PITCH, aux), F32),
            pltpu.VMEM((times * NO, 2 * NO, aux), BF16),
            pltpu.VMEM((NO * aux, times * 2 * NO), BF16),
            pltpu.VMEM((times * aux, aux), BF16),
            pltpu.VMEM((times * aux, NO * NO), BF16),
            pltpu.VMEM(green.shape, F32),
            pltpu.VMEM((steps, *block), BF16),
            pltpu.VMEM((steps, cols_n, *block), BF16),
            pltpu.VMEM((steps, rows_n, *block), BF16),
            pltpu.VMEM((steps, rows_n, *block), BF16),
            pltpu.SemaphoreType.DMA((steps, cols_n)),
            pltpu.SemaphoreType.DMA((steps, cols_n)),
            pltpu.SemaphoreType.DMA((steps, rows_n)),
            pltpu.SemaphoreType.DMA((steps, rows_n)),
        ],
        compiler_params=pltpu.CompilerParams(
            collective_id=0, has_side_effects=True, vmem_limit_bytes=62 << 20
        ),
        name="whole",
    )(green, fit, stacked)


def solution(mesh):
    in_specs = (P("groups", None, ("row", "col")), P("groups", None), P("groups", "row", "col"))
    out_specs = P("groups", None, ("row", "col"))
    return jax.shard_map(local, mesh=mesh, in_specs=in_specs, out_specs=out_specs, check_vma=False)
```

profile of v0, /device:TPU:3, one launch (start us, length us, event | category | flops | bytes accessed | tf_op | source)
XLA Modules:
  0.0 54.9 jit_solution(2022192099220060254)
XLA Ops:
  0.0 53.3 %whole.1 = f32[2,128,128]{2,1,0:T(8,128)} custom-call(f32[2,128,128]{2,1,0:T(8,128)} %green_ref.1, bf16[128,4096]{1,0:T(8,128)(2,1)} %fit_ref.1, bf16[1024,512]{1,0:T(8,128)(2,1)} %bitcast.1), custom_call_target="tpu_custom_call" | custom-call | tf_op jit(solution)/shard_map/whole/pallas_call | solution.py:255
  53.3 1.6 %copy.5 = f32[2,128,128]{2,1,0:T(8,128)} copy(f32[2,128,128]{2,1,0:T(8,128)} %whole.1) | data formatting | bytes 262144
where the time goes:
time: 55.1 us; the launch traced here: 54.9 us
  Pallas kernels  53.3 us (97%)
  local copies, waits for them, and re-layouts  1.57 us (3%)
    pallas_call x1, Pallas kernels, local(): pl.pallas_call(functools.partial(whole_kernel, rows_n, cols_n), out_shape...  53.3 us
    unnamed x1, local copies, waits for them, and re-layouts  1.57 us

commit v1 on v0

v1 whole, which is shorter than its diff:
```python
import functools

import jax
import jax.numpy as jnp
from jax import lax
from jax.experimental import pallas as pl
from jax.experimental.pallas import tpu as pltpu
from jax.sharding import PartitionSpec as P

NO = 64
NEW = 2
ITERS = 2
PITCH = NO + 8
SLOTS = 4
PAIR = 2 * NO
WIDE = SLOTS * NO
F32 = jnp.float32
BF16 = jnp.bfloat16
MESH = pl.DeviceIdType.MESH
VMEM = pl.BlockSpec(memory_space=pltpu.VMEM)


def mm(a, b):
    return jnp.dot(a, b, preferred_element_type=F32)


def mm_nt(a, b):
    return lax.dot_general(a, b, (((1,), (1,)), ((), ())), preferred_element_type=F32)


def prepare(fit_ref, fitt_ref, bt_ref, turned):
    for pair in range(NO // 2):
        at = slice(pair * PAIR, (pair + 1) * PAIR)
        block = fit_ref[:, at].astype(F32).T
        fitt_ref[at, :] = block.astype(BF16)
        for half in range(2):
            i = 2 * pair + half
            turned[i * PITCH : i * PITCH + NO, :] = block[half * NO : (half + 1) * NO]
    for pair in range(NO // 2):
        pieces = [turned[pl.ds(2 * pair + half, NO, stride=PITCH), :] for half in range(2)]
        bt_ref[:, pair * PAIR : (pair + 1) * PAIR] = jnp.concatenate(pieces, axis=0).T.astype(BF16)


def places(sel_ref):
    shape = (PAIR, 2 * PAIR)
    row = lax.broadcasted_iota(jnp.int32, shape, 0)
    lane = lax.broadcasted_iota(jnp.int32, shape, 1)
    c, i = row // NO, row % NO
    for q in range(2):
        k = c * PAIR + (i // SLOTS) * (2 * SLOTS) + q * SLOTS + i % SLOTS
        sel_ref[q] = jnp.where(lane == k, 1.0, 0.0).astype(BF16)


def lay_out(a, now_ref, sel_ref, slotted, slot_ref, turn_ref):
    span = now_ref.shape[2]
    rows = 2 * span * SLOTS
    lane = lax.broadcasted_iota(jnp.int32, (span, PAIR), 1)
    blocks = [now_ref[c, a * NO : (a + 1) * NO, :] for c in range(2)]
    for c in range(2):
        both = jnp.concatenate([blocks[c], blocks[c]], axis=0).T
        halves = [jnp.where(lane < NO, both, 0.0), jnp.where(lane >= NO, both, 0.0)]
        for s in range(SLOTS):
            slotted[pl.ds((s // 2) * rows + c * span * SLOTS + s, span, stride=SLOTS), :] = halves[s % 2]
    for half in range(2):
        slot_ref[:, half * PAIR : (half + 1) * PAIR] = slotted[half * rows : (half + 1) * rows, :].astype(BF16)
    turned = jnp.concatenate(blocks, axis=0).T.astype(BF16)
    for q in range(2):
        turn_ref[q] = mm(turned, sel_ref[q]).astype(BF16)


def left(fit_ref, slot_ref, m_ref):
    aux = fit_ref.shape[0]
    for t in range(NO // (2 * SLOTS)):
        at = 2 * t * WIDE
        weights = jnp.concatenate([fit_ref[:, at : at + WIDE], fit_ref[:, at + WIDE : at + 2 * WIDE]], axis=0)
        res = mm_nt(slot_ref[...], weights)
        parts = [res[:, h * aux : (h + 1) * aux].reshape(-1, 2 * SLOTS, aux) for h in range(2)]
        m_ref[:, 4 * SLOTS * t : 4 * SLOTS * (t + 1), :] = jnp.concatenate(parts, axis=1).astype(BF16)


def pair_tile(m_ref, times, n, pair):
    pairs = NO // 2
    return jnp.concatenate([m_ref[(c * times + n) * pairs + pair] for c in range(2)], axis=0)


def contract(times, fitt_ref, bt_ref, sel_ref, turn_ref, m_ref, x_ref, w_ref):
    aux = fitt_ref.shape[1]
    for n in range(times):
        lhs = jnp.concatenate([turn_ref[q, n * NO : (n + 1) * NO, :] for q in range(2)], axis=0)
        for u in range(NO // 4):
            pairs = [2 * u, 2 * u + 1]
            res = mm(lhs, jnp.concatenate([pair_tile(m_ref, times, n, p) for p in pairs], axis=1)).astype(BF16)
            for d, p in enumerate(pairs):
                x_ref[p * PAIR : (p + 1) * PAIR, n * aux : (n + 1) * aux] = res[:, d * aux : (d + 1) * aux]

    pi = (mm(bt_ref[...], x_ref[...]) * (1.0 / NO)).astype(BF16)

    for step in range(NO * NO // 512):
        at = slice(step * 512, (step + 1) * 512)
        w_ref[at, :] = mm(fitt_ref[at, :], pi).astype(BF16)

    scale = (aux * NO) ** (-0.5)
    lane = lax.broadcasted_iota(jnp.int32, (NO, 2 * PAIR), 1)
    first = lane % (2 * SLOTS) < SLOTS
    sums = []
    for n in range(times):
        lanes = slice(n * aux, (n + 1) * aux)
        acc = jnp.zeros((PAIR, 2 * PAIR), F32)
        for u in range(NO // 4):
            pairs = [2 * u, 2 * u + 1]
            lhs = jnp.concatenate([w_ref[p * PAIR : (p + 1) * PAIR, lanes] for p in pairs], axis=1)
            rhs = jnp.concatenate([pair_tile(m_ref, times, n, p) for p in pairs], axis=1)
            acc = acc + mm_nt(lhs, rhs)
        sums.append(jnp.where(first, acc[:NO], acc[NO:]))
    total = jnp.concatenate(sums, axis=0) * scale
    high = total.astype(BF16)
    low = (total - high.astype(F32)).astype(BF16)
    fold = sel_ref[0] + sel_ref[1]
    return (mm_nt(fold, high) + mm_nt(fold, low)).astype(BF16)


def whole_kernel(
    rows_n, cols_n, green_ref, fit_ref, hist_ref, out_ref,
    fitt, bt, turned, sel, slotted, slot_ref, turn_ref, m_ref, x_ref, w_ref,
    now, energy, seg, part, got, gs_sem, gr_sem, ss_sem, sr_sem,
):
    row, col = lax.axis_index("row"), lax.axis_index("col")
    span = green_ref.shape[2]
    times = span // NO
    source_col = (row * cols_n + col) // rows_n

    def owner(m):
        t = col * rows_n + m
        return t // cols_n, lax.rem(t, cols_n)

    def away(m):
        to_row, to_col = owner(m)
        return jnp.logical_or(to_row != row, to_col != col)

    def foreign(r):
        return jnp.logical_or(row != r, col != source_col)

    def place(r, c):
        return {"row": r, "col": c}

    barrier = pltpu.get_barrier_semaphore()
    for d in range(1, cols_n):
        pl.semaphore_signal(barrier, inc=1, device_id=place(row, lax.rem(col + d, cols_n)), device_id_type=MESH)
    for r in range(rows_n):

        @pl.when(foreign(r))
        def _():
            pl.semaphore_signal(barrier, inc=1, device_id=place(r, source_col), device_id_type=MESH)

    slotted[...] = jnp.zeros_like(slotted)
    places(sel)
    prepare(fit_ref, fitt, bt, turned)

    keeps = jnp.where(source_col == col, 1, 0)
    pl.semaphore_wait(barrier, cols_n - 1 + rows_n - keeps)

    def gather(s, d):
        return pltpu.make_async_remote_copy(
            src_ref=energy.at[s],
            dst_ref=seg.at[s, col],
            send_sem=gs_sem.at[s, d],
            recv_sem=gr_sem.at[s, d],
            device_id=place(row, lax.rem(col + d, cols_n)),
            device_id_type=MESH,
        )

    def scatter(s, m):
        return pltpu.make_async_remote_copy(
            src_ref=part.at[s, m],
            dst_ref=got.at[s, row],
            send_sem=ss_sem.at[s, m],
            recv_sem=sr_sem.at[s, row],
            device_id=place(*owner(m)),
            device_id_type=MESH,
        )

    def arriving(s, r):
        return pltpu.make_async_remote_copy(
            src_ref=part.at[s, r],
            dst_ref=got.at[s, r],
            send_sem=ss_sem.at[s, r],
            recv_sem=sr_sem.at[s, r],
            device_id=place(r, source_col),
            device_id_type=MESH,
        )

    def keep(s, m):
        return pltpu.make_async_copy(part.at[s, m], got.at[s, row], sr_sem.at[s, row])

    def multiply(s):
        for d in range(1, cols_n):
            gather(s, d).wait_recv()
        real = [seg[s, q, :NO, :] for q in range(cols_n)]
        imag = [seg[s, q, NO:, :] for q in range(cols_n)]
        lhs = jnp.concatenate(
            [jnp.concatenate(real + [-x for x in imag], axis=1), jnp.concatenate(imag + real, axis=1)], axis=0
        )
        for m in range(rows_n):
            part[s, m] = mm(lhs, hist_ref[:, m * span : (m + 1) * span]).astype(BF16)
        for m in range(rows_n):

            @pl.when(away(m))
            def _():
                scatter(s, m).start()

            @pl.when(jnp.logical_not(away(m)))
            def _():
                keep(s, m).start()

    def collect(s, target):
        a = s % NEW
        for r in range(rows_n):

            @pl.when(foreign(r))
            def _():
                arriving(s, r).wait_recv()

            @pl.when(jnp.logical_not(foreign(r)))
            def _():
                keep(s, r).wait()

        total = got[s, 0].astype(F32)
        for r in range(1, rows_n):
            total = total + got[s, r].astype(F32)
        for c in range(2):
            at = slice(a * NO, (a + 1) * NO)
            target[c, at, :] = green_ref[c, at, :] + total[c * NO : (c + 1) * NO]

    steps = ITERS * NEW
    for s in range(steps):
        a = s % NEW
        if s >= NEW:
            collect(s - NEW, now)
        lay_out(a, green_ref if s < NEW else now, sel, slotted, slot_ref, turn_ref)
        left(fit_ref, slot_ref, m_ref)
        if s >= 1:
            multiply(s - 1)
        value = contract(times, fitt, bt, sel, turn_ref, m_ref, x_ref, w_ref)
        energy[s] = value
        for d in range(1, cols_n):
            gather(s, d).start()
        seg[s, col] = value
    multiply(steps - 1)
    for s in range(steps - NEW, steps):
        collect(s, out_ref)
    for s in range(steps):
        for d in range(1, cols_n):
            gather(s, d).wait_send()
        for m in range(rows_n):

            @pl.when(away(m))
            def _():
                scatter(s, m).wait_send()


def local(green, fit, history):
    rows_n, cols_n = lax.axis_size("row"), lax.axis_size("col")
    aux = fit.shape[0]
    span = green.shape[2]
    times = span // NO
    steps = ITERS * NEW
    stacked = history.reshape(2 * history.shape[1], history.shape[2])
    block = (2 * NO, span)
    return pl.pallas_call(
        functools.partial(whole_kernel, rows_n, cols_n),
        out_shape=jax.ShapeDtypeStruct(green.shape, F32),
        in_specs=[VMEM] * 3,
        out_specs=VMEM,
        scratch_shapes=[
            pltpu.VMEM((NO * NO, aux), BF16),
            pltpu.VMEM((aux, NO * NO), BF16),
            pltpu.VMEM((NO * PITCH, aux), F32),
            pltpu.VMEM((2, PAIR, 2 * PAIR), BF16),
            pltpu.VMEM((2 * 2 * span * SLOTS, PAIR), F32),
            pltpu.VMEM((2 * span * SLOTS, WIDE), BF16),
            pltpu.VMEM((2, span, 2 * PAIR), BF16),
            pltpu.VMEM((span, PAIR, aux), BF16),
            pltpu.VMEM((NO * NO, times * aux), BF16),
            pltpu.VMEM((NO * NO, times * aux), BF16),
            pltpu.VMEM(green.shape, F32),
            pltpu.VMEM((steps, *block), BF16),
            pltpu.VMEM((steps, cols_n, *block), BF16),
            pltpu.VMEM((steps, rows_n, *block), BF16),
            pltpu.VMEM((steps, rows_n, *block), BF16),
            pltpu.SemaphoreType.DMA((steps, cols_n)),
            pltpu.SemaphoreType.DMA((steps, cols_n)),
            pltpu.SemaphoreType.DMA((steps, rows_n)),
            pltpu.SemaphoreType.DMA((steps, rows_n)),
        ],
        compiler_params=pltpu.CompilerParams(
            collective_id=0, has_side_effects=True, vmem_limit_bytes=62 << 20
        ),
        name="whole",
    )(green, fit, stacked)


def solution(mesh):
    in_specs = (P("groups", None, ("row", "col")), P("groups", None), P("groups", "row", "col"))
    out_specs = P("groups", None, ("row", "col"))
    return jax.shard_map(local, mesh=mesh, in_specs=in_specs, out_specs=out_specs, check_vma=False)
```

time: 55.1 us -> 49.7 us (0.902)
  Pallas kernels: 53.3 us -> 47.9 us
    pallas_call x1, Pallas kernels: 53.3 us -> 47.9 us  [local(): pl.pallas_call(functools.partial(whole_kernel, rows_n, cols_n), out_shape...]
where the time goes in v1:
time: 49.7 us; the launch traced here: 49.5 us
  Pallas kernels  47.9 us (96%)
  local copies, waits for them, and re-layouts  1.57 us (3%)
    pallas_call x1, Pallas kernels, local(): pl.pallas_call(functools.partial(whole_kernel, rows_n, cols_n), out_shape...  47.9 us
    unnamed x1, local copies, waits for them, and re-layouts  1.57 us

profile of v1, /device:TPU:3, one launch (start us, length us, event | category | flops | bytes accessed | tf_op | source)
XLA Modules:
  0.0 49.5 jit_solution(1005954731052536183)
XLA Ops:
  0.0 47.9 %whole.1 = f32[2,128,128]{2,1,0:T(8,128)} custom-call(f32[2,128,128]{2,1,0:T(8,128)} %green_ref.1, bf16[128,4096]{1,0:T(8,128)(2,1)} %fit_ref.1, bf16[1024,512]{1,0:T(8,128)(2,1)} %bitcast.1), custom_call_target="tpu_custom_call" | custom-call | tf_op jit(solution)/shard_map/whole/pallas_call | solution.py:269
  48.0 1.6 %copy.5 = f32[2,128,128]{2,1,0:T(8,128)} copy(f32[2,128,128]{2,1,0:T(8,128)} %whole.1) | data formatting | bytes 262144

commit v2 on v1

--- a/solution.py
+++ b/solution.py
@@ -14,6 +14,7 @@
 SLOTS = 4
 PAIR = 2 * NO
 WIDE = SLOTS * NO
+LEFTS = NO // (2 * SLOTS)
 F32 = jnp.float32
 BF16 = jnp.bfloat16
 MESH = pl.DeviceIdType.MESH
@@ -28,17 +29,21 @@
     return lax.dot_general(a, b, (((1,), (1,)), ((), ())), preferred_element_type=F32)
 
 
-def prepare(fit_ref, fitt_ref, bt_ref, turned):
-    for pair in range(NO // 2):
-        at = slice(pair * PAIR, (pair + 1) * PAIR)
-        block = fit_ref[:, at].astype(F32).T
-        fitt_ref[at, :] = block.astype(BF16)
-        for half in range(2):
-            i = 2 * pair + half
-            turned[i * PITCH : i * PITCH + NO, :] = block[half * NO : (half + 1) * NO]
-    for pair in range(NO // 2):
-        pieces = [turned[pl.ds(2 * pair + half, NO, stride=PITCH), :] for half in range(2)]
-        bt_ref[:, pair * PAIR : (pair + 1) * PAIR] = jnp.concatenate(pieces, axis=0).T.astype(BF16)
+def prepare(piece, pieces, fit_ref, fitt_ref, bt_ref, turned):
+    half_way = pieces // 2
+    share = NO // 2 // half_way
+    if piece < half_way:
+        for pair in range(piece * share, (piece + 1) * share):
+            at = slice(pair * PAIR, (pair + 1) * PAIR)
+            block = fit_ref[:, at].astype(F32).T
+            fitt_ref[at, :] = block.astype(BF16)
+            for half in range(2):
+                i = 2 * pair + half
+                turned[i * PITCH : i * PITCH + NO, :] = block[half * NO : (half + 1) * NO]
+        return
+    for pair in range((piece - half_way) * share, (piece - half_way + 1) * share):
+        rows = [turned[pl.ds(2 * pair + half, NO, stride=PITCH), :] for half in range(2)]
+        bt_ref[:, pair * PAIR : (pair + 1) * PAIR] = jnp.concatenate(rows, axis=0).T.astype(BF16)
 
 
 def places(sel_ref):
@@ -68,14 +73,16 @@
         turn_ref[q] = mm(turned, sel_ref[q]).astype(BF16)
 
 
-def left(fit_ref, slot_ref, m_ref):
+def left(fit_ref, slot_ref, m_ref, beside):
     aux = fit_ref.shape[0]
-    for t in range(NO // (2 * SLOTS)):
+    for t in range(LEFTS):
         at = 2 * t * WIDE
         weights = jnp.concatenate([fit_ref[:, at : at + WIDE], fit_ref[:, at + WIDE : at + 2 * WIDE]], axis=0)
         res = mm_nt(slot_ref[...], weights)
         parts = [res[:, h * aux : (h + 1) * aux].reshape(-1, 2 * SLOTS, aux) for h in range(2)]
         m_ref[:, 4 * SLOTS * t : 4 * SLOTS * (t + 1), :] = jnp.concatenate(parts, axis=1).astype(BF16)
+        if beside is not None:
+            beside(t)
 
 
 def pair_tile(m_ref, times, n, pair):
@@ -83,8 +90,8 @@
     return jnp.concatenate([m_ref[(c * times + n) * pairs + pair] for c in range(2)], axis=0)
 
 
-def contract(times, fitt_ref, bt_ref, sel_ref, turn_ref, m_ref, x_ref, w_ref):
-    aux = fitt_ref.shape[1]
+def polarise(times, bt_ref, turn_ref, m_ref, x_ref):
+    aux = bt_ref.shape[0]
     for n in range(times):
         lhs = jnp.concatenate([turn_ref[q, n * NO : (n + 1) * NO, :] for q in range(2)], axis=0)
         for u in range(NO // 4):
@@ -93,8 +100,11 @@
             for d, p in enumerate(pairs):
                 x_ref[p * PAIR : (p + 1) * PAIR, n * aux : (n + 1) * aux] = res[:, d * aux : (d + 1) * aux]
 
-    pi = (mm(bt_ref[...], x_ref[...]) * (1.0 / NO)).astype(BF16)
-
+    return (mm(bt_ref[...], x_ref[...]) * (1.0 / NO)).astype(BF16)
+
+
+def dress(times, pi, fitt_ref, sel_ref, m_ref, w_ref):
+    aux = fitt_ref.shape[1]
     for step in range(NO * NO // 512):
         at = slice(step * 512, (step + 1) * 512)
         w_ref[at, :] = mm(fitt_ref[at, :], pi).astype(BF16)
@@ -120,7 +130,7 @@
 
 
 def whole_kernel(
-    rows_n, cols_n, green_ref, fit_ref, hist_ref, out_ref,
+    rows_n, cols_n, green_ref, fit_ref, hist_hbm, out_ref, hist_ref, load_sem,
     fitt, bt, turned, sel, slotted, slot_ref, turn_ref, m_ref, x_ref, w_ref,
     now, energy, seg, part, got, gs_sem, gr_sem, ss_sem, sr_sem,
 ):
@@ -152,12 +162,10 @@
         def _():
             pl.semaphore_signal(barrier, inc=1, device_id=place(r, source_col), device_id_type=MESH)
 
+    load = pltpu.make_async_copy(hist_hbm, hist_ref, load_sem)
+    load.start()
     slotted[...] = jnp.zeros_like(slotted)
     places(sel)
-    prepare(fit_ref, fitt, bt, turned)
-
-    keeps = jnp.where(source_col == col, 1, 0)
-    pl.semaphore_wait(barrier, cols_n - 1 + rows_n - keeps)
 
     def gather(s, d):
         return pltpu.make_async_remote_copy(
@@ -200,8 +208,11 @@
         lhs = jnp.concatenate(
             [jnp.concatenate(real + [-x for x in imag], axis=1), jnp.concatenate(imag + real, axis=1)], axis=0
         )
-        for m in range(rows_n):
-            part[s, m] = mm(lhs, hist_ref[:, m * span : (m + 1) * span]).astype(BF16)
+        group = 2 if rows_n % 2 == 0 else 1
+        for m in range(0, rows_n, group):
+            value = mm(lhs, hist_ref[:, m * span : (m + group) * span]).astype(BF16)
+            for d in range(group):
+                part[s, m + d] = value[:, d * span : (d + 1) * span]
         for m in range(rows_n):
 
             @pl.when(away(m))
@@ -231,17 +242,28 @@
             at = slice(a * NO, (a + 1) * NO)
             target[c, at, :] = green_ref[c, at, :] + total[c * NO : (c + 1) * NO]
 
+    def beside(t):
+        prepare(t, LEFTS, fit_ref, fitt, bt, turned)
+
     steps = ITERS * NEW
     for s in range(steps):
         a = s % NEW
         if s >= NEW:
+            if a == 0:
+                multiply(s - 1)
             collect(s - NEW, now)
         lay_out(a, green_ref if s < NEW else now, sel, slotted, slot_ref, turn_ref)
-        left(fit_ref, slot_ref, m_ref)
-        if s >= 1:
+        left(fit_ref, slot_ref, m_ref, beside if s == 0 else None)
+        pi = polarise(times, bt, turn_ref, m_ref, x_ref)
+        if a > 0:
+            if s == 1:
+                load.wait()
             multiply(s - 1)
-        value = contract(times, fitt, bt, sel, turn_ref, m_ref, x_ref, w_ref)
+        value = dress(times, pi, fitt, sel, m_ref, w_ref)
         energy[s] = value
+        if s == 0:
+            keeps = jnp.where(source_col == col, 1, 0)
+            pl.semaphore_wait(barrier, cols_n - 1 + rows_n - keeps)
         for d in range(1, cols_n):
             gather(s, d).start()
         seg[s, col] = value
@@ -269,9 +291,11 @@
     return pl.pallas_call(
         functools.partial(whole_kernel, rows_n, cols_n),
         out_shape=jax.ShapeDtypeStruct(green.shape, F32),
-        in_specs=[VMEM] * 3,
+        in_specs=[VMEM, VMEM, pl.BlockSpec(memory_space=pl.ANY)],
         out_specs=VMEM,
         scratch_shapes=[
+            pltpu.VMEM(stacked.shape, BF16),
+            pltpu.SemaphoreType.DMA,
             pltpu.VMEM((NO * NO, aux), BF16),
             pltpu.VMEM((aux, NO * NO), BF16),
             pltpu.VMEM((NO * PITCH, aux), F32),

time: 49.7 us -> 45.2 us (0.909)
  Pallas kernels: 47.9 us -> 43.5 us
    pallas_call x1, Pallas kernels: 47.9 us -> 43.5 us  [local(): pl.pallas_call(functools.partial(whole_kernel, rows_n, cols_n), out_shape...]
where the time goes in v2:
time: 45.2 us; the launch traced here: 45.1 us
  Pallas kernels  43.5 us (96%)
  local copies, waits for them, and re-layouts  1.57 us (3%)
    pallas_call x1, Pallas kernels, local(): pl.pallas_call(functools.partial(whole_kernel, rows_n, cols_n), out_shape...  43.5 us
    unnamed x1, local copies, waits for them, and re-layouts  1.57 us

profile of v2, /device:TPU:3, one launch (start us, length us, event | category | flops | bytes accessed | tf_op | source)
XLA Modules:
  0.0 45.1 jit_solution(16662102897080260807)
XLA Ops:
  0.0 43.5 %whole.1 = f32[2,128,128]{2,1,0:T(8,128)} custom-call(f32[2,128,128]{2,1,0:T(8,128)} %green_ref.1, bf16[128,4096]{1,0:T(8,128)(2,1)} %fit_ref.1, bf16[1024,512]{1,0:T(8,128)(2,1)} %bitcast.1), custom_call_target="tpu_custom_call" | custom-call | tf_op jit(solution)/shard_map/whole/pallas_call | solution.py:291
  43.5 1.6 %copy.5 = f32[2,128,128]{2,1,0:T(8,128)} copy(f32[2,128,128]{2,1,0:T(8,128)} %whole.1) | data formatting | bytes 262144

commit v3 on v2

--- a/solution.py
+++ b/solution.py
@@ -100,7 +100,9 @@
             for d, p in enumerate(pairs):
                 x_ref[p * PAIR : (p + 1) * PAIR, n * aux : (n + 1) * aux] = res[:, d * aux : (d + 1) * aux]
 
-    return (mm(bt_ref[...], x_ref[...]) * (1.0 / NO)).astype(BF16)
+    half = NO * NO // 2
+    value = mm(bt_ref[:, :half], x_ref[:half]) * (1.0 / NO) + mm(bt_ref[:, half:], x_ref[half:]) * (1.0 / NO)
+    return value.astype(BF16)
 
 
 def dress(times, pi, fitt_ref, sel_ref, m_ref, w_ref):
@@ -115,14 +117,18 @@
     sums = []
     for n in range(times):
         lanes = slice(n * aux, (n + 1) * aux)
-        acc = jnp.zeros((PAIR, 2 * PAIR), F32)
-        for u in range(NO // 4):
-            pairs = [2 * u, 2 * u + 1]
-            lhs = jnp.concatenate([w_ref[p * PAIR : (p + 1) * PAIR, lanes] for p in pairs], axis=1)
-            rhs = jnp.concatenate([pair_tile(m_ref, times, n, p) for p in pairs], axis=1)
-            acc = acc + mm_nt(lhs, rhs)
+        accs = []
+        for h in range(2):
+            acc = jnp.zeros((PAIR, 2 * PAIR), F32)
+            for u in range(h * NO // 8, (h + 1) * NO // 8):
+                pairs = [2 * u, 2 * u + 1]
+                lhs = jnp.concatenate([w_ref[p * PAIR : (p + 1) * PAIR, lanes] for p in pairs], axis=1)
+                rhs = jnp.concatenate([pair_tile(m_ref, times, n, p) for p in pairs], axis=1)
+                acc = acc + mm_nt(lhs, rhs)
+            accs.append(acc * scale)
+        acc = accs[0] + accs[1]
         sums.append(jnp.where(first, acc[:NO], acc[NO:]))
-    total = jnp.concatenate(sums, axis=0) * scale
+    total = jnp.concatenate(sums, axis=0)
     high = total.astype(BF16)
     low = (total - high.astype(F32)).astype(BF16)
     fold = sel_ref[0] + sel_ref[1]
@@ -205,15 +211,19 @@
             gather(s, d).wait_recv()
         real = [seg[s, q, :NO, :] for q in range(cols_n)]
         imag = [seg[s, q, NO:, :] for q in range(cols_n)]
-        lhs = jnp.concatenate(
-            [jnp.concatenate(real + [-x for x in imag], axis=1), jnp.concatenate(imag + real, axis=1)], axis=0
-        )
+        sides = [
+            jnp.concatenate([jnp.concatenate(real, axis=1), jnp.concatenate(imag, axis=1)], axis=0),
+            jnp.concatenate([jnp.concatenate(imag, axis=1), jnp.concatenate([-x for x in real], axis=1)], axis=0),
+        ]
+        depth = cols_n * span
         group = 2 if rows_n % 2 == 0 else 1
         for m in range(0, rows_n, group):
-            value = mm(lhs, hist_ref[:, m * span : (m + group) * span]).astype(BF16)
+            at = slice(m * span, (m + group) * span)
+            value = (mm(sides[0], hist_ref[:depth, at]) - mm(sides[1], hist_ref[depth:, at])).astype(BF16)
             for d in range(group):
                 part[s, m + d] = value[:, d * span : (d + 1) * span]
-        for m in range(rows_n):
+        for i in range(rows_n):
+            m = lax.rem(row + i, rows_n)
 
             @pl.when(away(m))
             def _():

time: 45.2 us -> 44.4 us (0.982)
  the two profiles are of different devices: /device:TPU:3 before, /device:TPU:0 now
where the time goes in v3:
time: 44.4 us; the launch traced here: 44.3 us
  Pallas kernels  42.7 us (96%)
  local copies, waits for them, and re-layouts  1.57 us (4%)
    pallas_call x1, Pallas kernels, local(): pl.pallas_call(functools.partial(whole_kernel, rows_n, cols_n), out_shape...  42.7 us
    unnamed x1, local copies, waits for them, and re-layouts  1.57 us

profile of v3, /device:TPU:0, one launch (start us, length us, event | category | flops | bytes accessed | tf_op | source)
XLA Modules:
  0.0 44.3 jit_solution(378110086969546273)
XLA Ops:
  0.0 42.7 %whole.1 = f32[2,128,128]{2,1,0:T(8,128)} custom-call(f32[2,128,128]{2,1,0:T(8,128)} %green_ref.1, bf16[128,4096]{1,0:T(8,128)(2,1)} %fit_ref.1, bf16[1024,512]{1,0:T(8,128)(2,1)} %bitcast.1), custom_call_target="tpu_custom_call" | custom-call | tf_op jit(solution)/shard_map/whole/pallas_call | solution.py:301
  42.7 1.6 %copy.5 = f32[2,128,128]{2,1,0:T(8,128)} copy(f32[2,128,128]{2,1,0:T(8,128)} %whole.1) | data formatting | bytes 262144
